TPU v7x, 256 devices: a whole 4x4x8 slice. The times are simulated.
256 devices in a mesh: blk: 32 (over x, z), leaf: 4 (over y), samp: 2 (over core).
Axes of the slice: x: 4, y: 4, z: 8, core: 2. Of those that a mesh axis runs over, the one named last changes fastest.
Arguments:
- points: float32 [3, 32768], P(None, ('blk', 'leaf')), may hold values from 0 to 64, as said below
- neighbors: int32 [128, 8], P(('blk', 'leaf')), may hold values from -1 to 127, as said below
- omega: float32 [512, 32768], P(None, ('blk', 'leaf')), may hold values from -6 to 6
- observed: float32 [32768], P(('blk', 'leaf')), may hold values from -6 to 6
- prior_draws: float32 [64, 32768], P('samp', ('blk', 'leaf')), may hold values from -6 to 6
Outputs:
- weights: float32 [64, 32768], P('samp', ('blk', 'leaf'))
- residual: float32 [64, 32768], P('samp', ('blk', 'leaf'))
Inputs may be any that keep to these rules, and one draw needn't show every extreme that they name: Block g's points lie in the unit cell with integer corner (cx, cy, cz), where cx // 2 = g // 4 and 0 <= cy, cz < 3. `neighbors`: row g lists in ascending order every block h whose unit cell touches g's (cells at most one apart in every coordinate, the first taken periodic of period 2 * 32), which includes every block with a point within distance 1 of a point of g, followed by -1 in the unused slots; the relation is symmetric, and every listed block has a slab index h // 4 equal to or cyclically next to g // 4.
All inputs are finite; a program needn't handle non-finite values.
Results may differ from a plain program's by a relative error of at most 0.0003.
Values sent between devices are 32-bit elements; how exact they have to be, the bound alone decides.
A program may use at most 64 MiB of HBM per device.

v0:
```python
import jax
import jax.numpy as jnp
from jax import lax
from jax.sharding import PartitionSpec as P

PB = 256
ITERS = 2
support_radius = 0.8
noise_variance = 1.0
sketch_shift = 1.0
ALL_AXES = ("blk", "leaf", "samp")


def shifted_2(block, axis, distance):
    devices = range(lax.axis_size(axis))
    route = [((i - distance) % len(devices), i) for i in devices]
    return lax.ppermute(block, axis, route)


def wendland(row_points, column_points, period):
    offset = row_points[None, :, :, None] - column_points[:, :, None, :]
    half_period = 0.5 * period
    along_x = jnp.mod(offset[:, 0] + half_period, period) - half_period
    squared = along_x * along_x + offset[:, 1] * offset[:, 1] + offset[:, 2] * offset[:, 2]
    radius = jnp.sqrt(squared) / support_radius
    remain = jnp.maximum(1.0 - radius, 0.0)
    return remain**4 * (4.0 * radius + 1.0)


def high_dot(left, right):
    return jnp.dot(left, right, precision=lax.Precision.HIGHEST, preferred_element_type=jnp.float32)


def shifted(values, offset_by):
    return shifted_2(values, "blk", offset_by)


def beside_all(values):
    slab_values = lax.all_gather(values, "leaf", axis=1, tiled=True)
    return jnp.concatenate([shifted(slab_values, 1), slab_values, shifted(slab_values, -1)], axis=1)


def lower_solve(factor, values):
    return lax.linalg.triangular_solve(factor, values, left_side=True, lower=True)


def local(points, neighbors, omega, observed, prior_draws):
    blk_dev = neighbors.shape[0]
    cycle_count = lax.axis_size("blk")
    slab_blocks = blk_dev * lax.axis_size("leaf")
    period = 2.0 * cycle_count
    own_slab = lax.axis_index("blk")
    n_samp = lax.axis_size("samp")
    samp_idx = lax.axis_index("samp")
    usable = neighbors >= 0
    relative = jnp.mod(neighbors // slab_blocks - own_slab + 1, cycle_count)
    chosen = jnp.where(usable, relative * slab_blocks + jnp.mod(neighbors, slab_blocks), 0)
    usable_weight = usable.astype(jnp.float32)
    reach_points = beside_all(points)
    reach_blocks = reach_points.reshape(3, 3 * slab_blocks, PB).transpose(1, 0, 2)
    row_blocks = points.reshape(3, blk_dev, PB).transpose(1, 0, 2)
    kernel_tile = wendland(row_blocks[0], reach_blocks[chosen[0]], period)
    kernel_tile = kernel_tile * usable_weight[0][:, None, None]

    def apply_kernel(values):
        width = values.shape[0]
        reach = beside_all(values).reshape(width, 3 * slab_blocks, PB)
        picked = jnp.take(reach, chosen[0], axis=1)
        return jnp.einsum("cnj,nij->ci", picked, kernel_tile, precision=lax.Precision.HIGHEST)

    def slot(x):
        zeros = jnp.zeros((n_samp,) + x.shape, x.dtype)
        return lax.dynamic_update_index_in_dim(zeros, x, samp_idx, 0)

    def unslot(xs):
        return lax.dynamic_index_in_dim(xs, samp_idx, 0, keepdims=False)

    def total_per_samp(values):
        return jax.tree.map(unslot, lax.psum(jax.tree.map(slot, values), ALL_AXES))

    sketch = apply_kernel(omega) + sketch_shift * omega
    rhs = observed[None, :] - prior_draws
    half = PB // n_samp
    omega_half = lax.dynamic_slice_in_dim(omega, samp_idx * half, half, axis=1)
    sketch_half = lax.dynamic_slice_in_dim(sketch, samp_idx * half, half, axis=1)
    core_part = high_dot(omega_half, sketch_half.T)
    square_part = high_dot(sketch_half, sketch_half.T)
    joint_part = 0.5 * (core_part + core_part.T) + 0.5 * (square_part + square_part.T)
    rhs_part = slot(high_dot(sketch, rhs.T))
    joint_gram, rhs_proj = lax.psum((joint_part, rhs_part), ALL_AXES)
    rhs_proj = unslot(rhs_proj)
    joint_factor = jnp.linalg.cholesky(joint_gram)

    def precond_from(vectors, projected):
        first_solve = lower_solve(joint_factor, projected)
        solved = lax.linalg.triangular_solve(
            joint_factor, first_solve, left_side=True, lower=True, transpose_a=True
        )
        return (vectors - high_dot(solved.T, sketch)) / noise_variance

    residual = rhs
    projected = rhs_proj
    precond = precond_from(residual, projected)
    direction = precond
    weights = jnp.zeros_like(rhs)
    image = apply_kernel(direction) + noise_variance * direction
    inner_now, curvature, image_proj = total_per_samp(
        (
            jnp.sum(residual * precond, axis=1),
            jnp.sum(direction * image, axis=1),
            high_dot(sketch, image.T),
        )
    )
    step_size = inner_now / curvature
    weights = weights + step_size[:, None] * direction
    residual = residual - step_size[:, None] * image
    projected = projected - step_size[None, :] * image_proj
    precond = precond_from(residual, projected)
    inner_next = total_per_samp(jnp.sum(residual * precond, axis=1))
    direction = precond + (inner_next / inner_now)[:, None] * direction
    inner_now = inner_next
    image = apply_kernel(direction) + noise_variance * direction
    curvature = total_per_samp(jnp.sum(direction * image, axis=1))
    step_size = inner_now / curvature
    weights = weights + step_size[:, None] * direction
    residual = residual - step_size[:, None] * image
    return (weights, residual)


def solution(mesh):
    in_specs = (
        P(None, ("blk", "leaf")),
        P(("blk", "leaf"), None),
        P(None, ("blk", "leaf")),
        P(("blk", "leaf")),
        P("samp", ("blk", "leaf")),
    )
    out_specs = (P("samp", ("blk", "leaf")), P("samp", ("blk", "leaf")))
    return jax.shard_map(local, mesh=mesh, in_specs=in_specs, out_specs=out_specs, check_vma=False)
```

profile of v0, /device:TPU:1, one launch (start us, length us, event | category | flops | bytes accessed | tf_op | source)
XLA Modules:
  0.0 1005.4 jit_solution(9335899095662480256)
XLA Ops:
  7.2 2.0 copy.10
  9.3 10.5 %all_gather.13 = f32[3,1024]{1,0:T(4,128)S(1)} all-gather(f32[3,256]{1,0:T(4,128)} %param.11), channel_id=1, replica_groups=mesh['blk'=32,'leaf'=4,'samp'=2] {'leaf'}, dimensions={1}, use_global_device_ids=true | all-gather | bytes 15360 | tf_op jit(solution)/shard_map/all_gather | solution.py:39
  19.9 7.8 collective-permute-start.3
  27.6 19.4 %all-gather.2.cloned.1.call-done = f32[512,1024]{0,1:T(8,128)} async-done(((f32[512,256]{0,1:T(8,128)}), f32[512,1024]{0,1:T(8,128)}) %all-gather.2.cloned.1.call-update) | async-done | bytes 2097168 | tf_op jit(solution)/shard_map/all_gather | solution.py:39
  47.1 5.2 collective-permute-start.1
  55.7 2.6 multiply_multiply_fusion
  58.3 38.5 %collective-permute-done.1 = f32[512,1024]{0,1:T(8,128)} collective-permute-done((f32[512,1024]{0,1:T(8,128)}, f32[512,1024]{0,1:T(8,128)}, u32[]{:S(2)}, u32[]{:S(2)}) %collective-permute-start.1) | collective-permute-done | bytes 2097184 | tf_op jit(solution)/shard_map/ppermute | solution.py:17
  96.8 5.4 collective-permute-done
  102.2 5.6 pad_maximum_fusion
  107.8 6.5 copy.11
  114.3 5.6 gather_fusion
  119.9 5.5 fusion.17
  125.4 2.0 fusion.34
  127.3 2.0 fusion.32
  129.4 2.5 copy.13
  131.9 2.5 copy.14
  134.5 3.7 fusion.26
  139.7 250.3 %all-reduce.8.cloned.1.call-done = (f32[512,512]{1,0:T(8,128)}, f32[2,512,32]{1,2,0:T(8,128)}) async-done(((f32[512,512]{1,0:T(8,128)}, f32[2,512,32]{1,2,0:T(8,128)}), (f32[512,512]{1,0:T(8,128)}, f32[2,512,32]{1,2,0:T(8,128)})) %all-reduce.8.cloned.1.call-update) | async-done | bytes 1179664 | tf_op jit(solution)/shard_map/psum | solution.py:90
  390.8 2.6 copy.15
  393.4 1.8 fusion.24
  396.2 11.7 %cholesky.104 = f32[128,128]{1,0:T(8,128)S(1)} custom-call(f32[128,128]{1,0:T(8,128)S(1)} %cholesky.266), custom_call_target="Cholesky" | custom-call | tf_op jit(solution)/shard_map/jit(cholesky)/cholesky | solution.py:92
  407.9 9.8 custom-call.33
  418.9 2.0 constant_dynamic-update-slice_fusion
  422.1 11.7 %cholesky.217 = f32[128,128]{1,0:T(8,128)S(1)} custom-call(f32[128,128]{1,0:T(8,128)S(1)} %cholesky.270), custom_call_target="Cholesky" | custom-call | tf_op jit(solution)/shard_map/jit(cholesky)/cholesky | solution.py:92
  434.5 10.2 %custom-call.34 = f32[1,128,128]{1,2,0:T(8,128)S(1)} custom-call(f32[1,128,128]{2,1,0:T(8,128)S(1)} %get-tuple-element.61), custom_call_target="InvertDiagBlocksLowerTriangular" | custom-call | tf_op jit(solution)/shard_map/jit(cholesky)/cholesky | solution.py:92
  447.1 11.7 %cholesky.238 = f32[128,128]{1,0:T(8,128)S(1)} custom-call(f32[128,128]{1,0:T(8,128)S(1)} %cholesky.275), custom_call_target="Cholesky" | custom-call | tf_op jit(solution)/shard_map/jit(cholesky)/cholesky | solution.py:92
  460.2 9.8 custom-call.35
  472.3 11.7 %cholesky.255 = f32[128,128]{1,0:T(8,128)S(1)} custom-call(f32[128,128]{1,0:T(8,128)S(1)} %convolution_subtract_fusion.2), custom_call_target="Cholesky" | custom-call | tf_op jit(solution)/shard_map/jit(cholesky)/cholesky | solution.py:92
  488.6 2.5 select_select_fusion
  491.1 12.0 %while.8 = (s32[]{:T(128)}, f32[512,512]{1,0:T(8,128)}, s32[4,2]{0,1:T(2,128)S(1)}, f32[4,128,128]{2,1,0:T(8,128)S(1)}, s32[]{:T(128)}) while((s32[]{:T(128)}, f32[512,512]{1,0:T(8,128)}, s32[4,2]{0,1:T(2,128)S(1)}, f32[4,128,128]{2,1,0:T(8,128)S(1)}, s32[]{:T(128)}) %tuple.51), condition=%wide.while_cond.1, body=%wide.while_body.1.sunk | while | flops 2 | bytes 131189 | solution.py:96
  491.7 2.3 bitcast_dynamic-update-slice_fusion.2
  494.8 2.3 bitcast_dynamic-update-slice_fusion.2
  497.8 2.3 bitcast_dynamic-update-slice_fusion.2
  500.8 2.3 bitcast_dynamic-update-slice_fusion.2
  503.1 39.3 %custom-call.39 = f32[4,128,128]{1,2,0:T(8,128)S(1)} custom-call(f32[4,128,128]{2,1,0:T(8,128)S(1)} %get-tuple-element.34), custom_call_target="InvertDiagBlocksLowerTriangular" | custom-call | tf_op jit(solution)/shard_map/triangular_solve/custom-call.8 | solution.py:96
  551.2 9.2 all_gather.14
  560.4 5.0 collective-permute-start.5
  565.4 1.9 collective-permute-done.5
  567.4 5.2 collective-permute-done.4
  573.2 2.8 multiply_reduce_fusion.3
  577.5 76.1 %all-reduce.1 = (f32[2,32]{1,0:T(2,128)S(1)}, f32[2,32]{1,0:T(2,128)S(1)}) all-reduce(f32[2,32]{1,0:T(2,128)S(1)} %dynamic_update_slice.22, f32[2,32]{1,0:T(2,128)S(1)} %dynamic_update_slice.21), channel_id=1, replica_groups=mesh['blk'=32,'leaf'=4,'samp'=2] {'blk','leaf','samp'}, use_global_device_ids=true, to_apply=%region_13.17 | all-reduce | flops 128 | bytes 1024 | tf_op jit(solution)/shard_map/psum | solution.py:79
  653.7 161.9 %all-reduce.6.cloned.1.call-done = f32[2,512,32]{1,2,0:T(8,128)} async-done(((f32[2,512,32]{1,2,0:T(8,128)}), f32[2,512,32]{1,2,0:T(8,128)}) %all-reduce.6.cloned.1.call-update) | async-done | bytes 131088 | tf_op jit(solution)/shard_map/psum | solution.py:79
  825.4 75.9 %psum.54 = f32[2,32]{1,0:T(2,128)S(1)} all-reduce(f32[2,32]{1,0:T(2,128)S(1)} %dynamic_update_slice.24), channel_id=1, replica_groups=mesh['blk'=32,'leaf'=4,'samp'=2] {'blk','leaf','samp'}, use_global_device_ids=true, to_apply=%region_16.20 | all-reduce | flops 64 | bytes 512 | tf_op jit(solution)/shard_map/psum | solution.py:79
  901.4 9.1 all_gather.15
  912.1 2.4 collective-permute-done.7
  914.5 4.6 collective-permute-done.6
  919.7 2.0 multiply_reduce_fusion
  921.8 76.2 %psum.55 = f32[2,32]{1,0:T(2,128)S(1)} all-reduce(f32[2,32]{1,0:T(2,128)S(1)} %dynamic_update_slice.25), channel_id=1, replica_groups=mesh['blk'=32,'leaf'=4,'samp'=2] {'blk','leaf','samp'}, use_global_device_ids=true, to_apply=%region_18.22 | all-reduce | flops 64 | bytes 512 | tf_op jit(solution)/shard_map/psum | solution.py:79
  (128 shorter events, 44.1 us)
Async XLA Ops:
  7.2 39.9 %all-gather.2.cloned.1.call-start = ((), (), s32[]{:S(2)}) async-start(), calls=%async_computation | async-start | bytes 2621440 | tf_op jit(solution)/shard_map/all_gather | solution.py:39
  9.3 380.7 %all-reduce.8.cloned.1.call-start = ((), (), s32[]{:S(2)}) async-start(), calls=%async_computation.2 | async-start | bytes 2359296 | tf_op jit(solution)/shard_map/psum | solution.py:90
  19.9 33.9 %collective-permute-start.3 = (f32[3,1024]{1,0:T(4,128)S(1)}, f32[3,1024]{1,0:T(4,128)S(1)}, u32[]{:S(2)}, u32[]{:S(2)}) collective-permute-start(f32[3,1024]{1,0:T(4,128)S(1)} %all_gather.13), channel_id=1, source_target_pairs={{8,0},{16,8},{24,16},{32,24},{40,32},{48,40},{56,48},{64,56},{72,6... | collective-permute-start | bytes 36872 | tf_op jit(solution)/shard_map/ppermute | solution.py:17
  27.6 26.1 %collective-permute-start.2 = (f32[3,1024]{1,0:T(4,128)S(1)}, f32[3,1024]{1,0:T(4,128)S(1)}, u32[]{:S(2)}, u32[]{:S(2)}) collective-permute-start(f32[3,1024]{1,0:T(4,128)S(1)} %all_gather.13), channel_id=1, source_target_pairs={{248,0},{0,8},{8,16},{16,24},{24,32},{32,40},{40,48},{48,56},{56,6... | collective-permute-start | bytes 36872 | tf_op jit(solution)/shard_map/ppermute | solution.py:17
  47.1 49.8 %collective-permute-start.1 = (f32[512,1024]{0,1:T(8,128)}, f32[512,1024]{0,1:T(8,128)}, u32[]{:S(2)}, u32[]{:S(2)}) collective-permute-start(f32[512,1024]{0,1:T(8,128)} %all-gather.2.cloned.1.call-done), channel_id=1, source_target_pairs={{8,0},{16,8},{24,16},{32,24},{40,32},{48,40},{56,48},{64,56},{72,6... | collective-permute-start | bytes 6291464 | tf_op jit(solution)/shard_map/ppermute | solution.py:17
  52.2 50.0 %collective-permute-start = (f32[512,1024]{0,1:T(8,128)}, f32[512,1024]{0,1:T(8,128)}, u32[]{:S(2)}, u32[]{:S(2)}) collective-permute-start(f32[512,1024]{0,1:T(8,128)} %all-gather.2.cloned.1.call-done), channel_id=1, source_target_pairs={{248,0},{0,8},{8,16},{16,24},{24,32},{32,40},{40,48},{48,56},{56,6... | collective-permute-start | bytes 6291464 | tf_op jit(solution)/shard_map/ppermute | solution.py:17
  55.7 46.5 %copy-start.2 = (f32[512,1024]{0,1:T(8,128)S(1)}, f32[512,1024]{0,1:T(8,128)}, u32[]{:S(2)}) copy-start(f32[512,1024]{0,1:T(8,128)} %all-gather.2.cloned.1.call-done) | copy-start | bytes 6291460
  114.3 5.6 copy-start
  134.5 3.7 copy-start.5
  134.5 3.7 copy-start.10
  138.8 0.6 copy-start.7
  139.4 676.2 %all-reduce.6.cloned.1.call-start = ((), (), s32[]{:S(2)}) async-start(), calls=%async_computation.1 | async-start | bytes 262144 | tf_op jit(solution)/shard_map/psum | solution.py:79
  395.2 1.0 copy-start.1
  551.2 16.2 %copy-start.3 = (f32[32,256]{1,0:T(8,128)}, f32[32,256]{1,0:T(8,128)S(1)}, u32[]{:S(2)}) copy-start(f32[32,256]{1,0:T(8,128)S(1)} %convolution_subtract_fusion.4) | copy-start | bytes 98308
  560.4 7.0 collective-permute-start.5
  565.4 7.1 collective-permute-start.4
  573.2 80.4 %copy-start.6 = (f32[32,256]{1,0:T(8,128)S(1)}, f32[32,256]{1,0:T(8,128)}, u32[]{:S(2)}) copy-start(f32[32,256]{1,0:T(8,128)} %param.15) | copy-start | bytes 98308
  573.2 242.4 %copy-start.9 = (f32[2,512,32]{1,2,0:T(8,128)S(1)}, f32[2,512,32]{1,2,0:T(8,128)}, u32[]{:S(2)}) copy-start(f32[2,512,32]{1,2,0:T(8,128)} %get-tuple-element.50) | copy-start | bytes 393220
  576.1 325.3 %copy-start.4 = (f32[32,256]{1,0:T(8,128)S(1)}, f32[32,256]{1,0:T(8,128)}, u32[]{:S(2)}) copy-start(f32[32,256]{1,0:T(8,128)} %copy-done.3) | copy-start | bytes 98308
  576.7 0.7 copy-start.8
  910.5 4.0 collective-permute-start.7
  911.9 7.1 collective-permute-start.6
Sparse Core Ops, SparseCore 0:
  9.8 37.2 all-gather.1
  139.5 250.3 all-reduce.7
  577.5 238.0 all-reduce.5
where the time goes:
time: 1010 us
  waiting for transfers between devices  490 us (49%)
  blocking collectives  257 us (25%)
  other arithmetic  141 us (14%)
  matrix products  40.6 us (4%)
  local copies, waits for them, and re-layouts  40.1 us (4%)
  starting transfers between devices  20.1 us (2%)
  between operations  17.2 us (2%)
    psum x1, waiting for transfers between devices, local(): joint_gram, rhs_proj = lax.psum((joint_part, rhs_part), ALL_AXES)  250 us
    psum x3, blocking collectives, total_per_samp(): return jax.tree.map(unslot, lax.psum(jax.tree.map(slot, values), ALL_AXES))  228 us
    psum x1, waiting for transfers between devices, total_per_samp(): return jax.tree.map(unslot, lax.psum(jax.tree.map(slot, values), ALL_AXES))  162 us
    another operation x14, other arithmetic, local(): joint_factor = jnp.linalg.cholesky(joint_gram)  80.7 us
    ppermute x8, waiting for transfers between devices, shifted_2(): return lax.ppermute(block, axis, route)  57.9 us
    another operation x4, other arithmetic, precond_from(): lax.linalg.triangular_solve(joint_factor, first_solve, left_side=True, lo...  41.8 us
    all_gather x3, blocking collectives, beside_all(): slab_values = lax.all_gather(values, 'leaf', axis=1, tiled=True)  28.8 us
  transfers between devices with their start and end apart: 11, of which 9 were waited for; matrix products, arithmetic and copies ran while one was open for 1% of the time, Pallas kernels for 0%

commit v1 on v0

--- a/solution.py
+++ b/solution.py
@@ -36,7 +36,12 @@
 
 
 def beside_all(values):
-    slab_values = lax.all_gather(values, "leaf", axis=1, tiled=True)
+    ring = [values]
+    for hop in range(3):
+        ring.append(lax.ppermute(ring[-1], "leaf", [(dev, (dev + 1) % 4) for dev in range(4)]))
+    slab_values = jnp.roll(
+        jnp.concatenate(ring[::-1], axis=1), (lax.axis_index("leaf") + 1) * ring[0].shape[1], axis=1
+    )
     return jnp.concatenate([shifted(slab_values, 1), slab_values, shifted(slab_values, -1)], axis=1)
 
 

time: 1010 us -> 1030 us (1.020)
  waiting for transfers between devices: 490 us -> 512 us
  blocking collectives: 257 us -> 240 us
  starting transfers between devices: 20.1 us -> 34.4 us
    ppermute x0 -> x12, waiting for transfers between devices: none -> 52.6 us  [beside_all(): lax.ppermute(ring[-1], 'leaf', [(dev, (dev + 1) % 4) for dev in range(4)])]
    all_gather x3 -> x0, blocking collectives: 28.8 us -> none  [beside_all(): slab_values = lax.all_gather(values, 'leaf', axis=1, tiled=True)]
    all_gather x1 -> x0, waiting for transfers between devices: 19.4 us -> none  [beside_all(): slab_values = lax.all_gather(values, 'leaf', axis=1, tiled=True)]
    ppermute x8, waiting for transfers between devices: 57.9 us -> 42.9 us  [shifted_2(): return lax.ppermute(block, axis, route)]
    psum x3, blocking collectives: 228 us -> 240 us  [total_per_samp(): return jax.tree.map(unslot, lax.psum(jax.tree.map(slot, values), ALL_AXES))]
  transfers between devices with their start and end apart: 11 -> 22, of which waited for: 9 -> 15; matrix products, arithmetic and copies ran while one was open for 1% -> 1% of each run, Pallas kernels for 0% -> 0%
where the time goes in v1:
time: 1030 us; the launch traced here: 1020 us
  waiting for transfers between devices  512 us (50%)
  blocking collectives  240 us (23%)
  other arithmetic  140 us (14%)
  matrix products  40.6 us (4%)
  local copies, waits for them, and re-layouts  39.6 us (4%)
  starting transfers between devices  34.4 us (3%)
  between operations  17.8 us (2%)
    psum x1, waiting for transfers between devices, local(): joint_gram, rhs_proj = lax.psum((joint_part, rhs_part), ALL_AXES)  256 us
    psum x3, blocking collectives, total_per_samp(): return jax.tree.map(unslot, lax.psum(jax.tree.map(slot, values), ALL_AXES))  240 us
    psum x1, waiting for transfers between devices, total_per_samp(): return jax.tree.map(unslot, lax.psum(jax.tree.map(slot, values), ALL_AXES))  161 us
    another operation x14, other arithmetic, local(): joint_factor = jnp.linalg.cholesky(joint_gram)  80.4 us
    ppermute x12, waiting for transfers between devices, beside_all(): lax.ppermute(ring[-1], 'leaf', [(dev, (dev + 1) % 4) for dev in range(4)])  52.6 us
    ppermute x8, waiting for transfers between devices, shifted_2(): return lax.ppermute(block, axis, route)  42.9 us
    another operation x4, other arithmetic, precond_from(): lax.linalg.triangular_solve(joint_factor, first_solve, left_side=True, lo...  41.8 us
    ppermute x8, starting transfers between devices, shifted_2(): return lax.ppermute(block, axis, route)  24.8 us
  transfers between devices with their start and end apart: 22, of which 15 were waited for; matrix products, arithmetic and copies ran while one was open for 1% of the time, Pallas kernels for 0%

profile of v1, /device:TPU:1, one launch (start us, length us, event | category | flops | bytes accessed | tf_op | source)
XLA Modules:
  0.0 1024.6 jit_solution(8591914442298133993)
XLA Ops:
  8.5 2.2 collective-permute-start
  10.7 11.0 %collective-permute-done = f32[512,256]{0,1:T(8,128)S(1)} collective-permute-done((f32[512,256]{0,1:T(8,128)S(1)}, f32[512,256]{0,1:T(8,128)S(1)}, u32[]{:S(2)}, u32[]{:S(2)}) %collective-permute-start) | collective-permute-done | bytes 524320 | tf_op jit(solution)/shard_map/ppermute | solution.py:41
  26.1 8.1 collective-permute-done.5
  37.9 9.0 collective-permute-done.7
  48.8 3.9 collective-permute-start.3
  52.7 6.1 collective-permute-start.4
  59.0 5.0 collective-permute-start.9
  64.0 38.1 %collective-permute-done.8 = f32[3,1024]{1,0:T(4,128)S(1)} collective-permute-done((f32[3,1024]{1,0:T(4,128)S(1)}, f32[3,1024]{1,0:T(4,128)S(1)}, u32[]{:S(2)}, u32[]{:S(2)}) %collective-permute-start.8) | collective-permute-done | bytes 12320 | tf_op jit(solution)/shard_map/ppermute | solution.py:17
  103.3 2.6 multiply_multiply_fusion
  106.0 6.2 pad_maximum_fusion
  112.2 6.5 copy.13
  118.7 5.6 gather_fusion
  124.3 5.5 fusion.17
  133.7 2.6 copy.15
  136.3 2.6 copy.16
  138.9 3.7 fusion.26
  144.3 256.0 %all-reduce.8.cloned.1.call-done = (f32[512,512]{1,0:T(8,128)}, f32[2,512,32]{1,2,0:T(8,128)}) async-done(((f32[512,512]{1,0:T(8,128)}, f32[2,512,32]{1,2,0:T(8,128)}), (f32[512,512]{1,0:T(8,128)}, f32[2,512,32]{1,2,0:T(8,128)})) %all-reduce.8.cloned.1.call-update) | async-done | bytes 1179664 | tf_op jit(solution)/shard_map/psum | solution.py:95
  400.3 2.6 copy.17
  405.6 11.7 %cholesky.104 = f32[128,128]{1,0:T(8,128)S(1)} custom-call(f32[128,128]{1,0:T(8,128)S(1)} %cholesky.266), custom_call_target="Cholesky" | custom-call | tf_op jit(solution)/shard_map/jit(cholesky)/cholesky | solution.py:97
  418.5 9.8 custom-call.33
  431.5 11.7 %cholesky.217 = f32[128,128]{1,0:T(8,128)S(1)} custom-call(f32[128,128]{1,0:T(8,128)S(1)} %cholesky.270), custom_call_target="Cholesky" | custom-call | tf_op jit(solution)/shard_map/jit(cholesky)/cholesky | solution.py:97
  443.9 9.9 custom-call.34
  456.3 11.7 %cholesky.238 = f32[128,128]{1,0:T(8,128)S(1)} custom-call(f32[128,128]{1,0:T(8,128)S(1)} %cholesky.275), custom_call_target="Cholesky" | custom-call | tf_op jit(solution)/shard_map/jit(cholesky)/cholesky | solution.py:97
  469.3 9.8 custom-call.35
  481.4 11.7 %cholesky.255 = f32[128,128]{1,0:T(8,128)S(1)} custom-call(f32[128,128]{1,0:T(8,128)S(1)} %convolution_subtract_fusion.2), custom_call_target="Cholesky" | custom-call | tf_op jit(solution)/shard_map/jit(cholesky)/cholesky | solution.py:97
  497.6 2.5 select_select_fusion
  500.2 11.2 %while.8 = (s32[]{:T(128)}, f32[512,512]{1,0:T(8,128)}, s32[4,2]{0,1:T(2,128)S(1)}, f32[4,128,128]{2,1,0:T(8,128)S(1)}, s32[]{:T(128)}) while((s32[]{:T(128)}, f32[512,512]{1,0:T(8,128)}, s32[4,2]{0,1:T(2,128)S(1)}, f32[4,128,128]{2,1,0:T(8,128)S(1)}, s32[]{:T(128)}) %tuple.52), condition=%wide.while_cond.1, body=%wide.while_body.1.sunk | while | flops 2 | bytes 131181 | solution.py:101
  500.8 2.2 bitcast_dynamic-update-slice_fusion.2
  503.6 2.2 bitcast_dynamic-update-slice_fusion.2
  506.4 2.2 bitcast_dynamic-update-slice_fusion.2
  509.3 2.1 bitcast_dynamic-update-slice_fusion.2
  511.4 39.3 %custom-call.39 = f32[4,128,128]{1,2,0:T(8,128)S(1)} custom-call(f32[4,128,128]{2,1,0:T(8,128)S(1)} %get-tuple-element.35), custom_call_target="InvertDiagBlocksLowerTriangular" | custom-call | tf_op jit(solution)/shard_map/triangular_solve/custom-call.8 | solution.py:101
  560.8 2.9 collective-permute-done.10
  563.7 4.6 collective-permute-done.11
  568.3 4.0 collective-permute-done.12
  572.4 4.8 collective-permute-start.14
  577.2 2.3 collective-permute-done.13
  580.2 2.8 multiply_reduce_fusion.3
  584.4 83.4 %all-reduce.1 = (f32[2,32]{1,0:T(2,128)S(1)}, f32[2,32]{1,0:T(2,128)S(1)}) all-reduce(f32[2,32]{1,0:T(2,128)S(1)} %dynamic_update_slice.22, f32[2,32]{1,0:T(2,128)S(1)} %dynamic_update_slice.21), channel_id=1, replica_groups=mesh['blk'=32,'leaf'=4,'samp'=2] {'blk','leaf','samp'}, use_global_device_ids=true, to_apply=%region_13.18 | all-reduce | flops 128 | bytes 1024 | tf_op jit(solution)/shard_map/psum | solution.py:84
  667.9 160.6 %all-reduce.6.cloned.1.call-done = f32[2,512,32]{1,2,0:T(8,128)} async-done(((f32[2,512,32]{1,2,0:T(8,128)}), f32[2,512,32]{1,2,0:T(8,128)}) %all-reduce.6.cloned.1.call-update) | async-done | bytes 131088 | tf_op jit(solution)/shard_map/psum | solution.py:84
  838.3 75.9 %psum.54 = f32[2,32]{1,0:T(2,128)S(1)} all-reduce(f32[2,32]{1,0:T(2,128)S(1)} %dynamic_update_slice.24), channel_id=1, replica_groups=mesh['blk'=32,'leaf'=4,'samp'=2] {'blk','leaf','samp'}, use_global_device_ids=true, to_apply=%region_16.21 | all-reduce | flops 64 | bytes 512 | tf_op jit(solution)/shard_map/psum | solution.py:84
  914.4 4.0 collective-permute-done.15
  918.3 4.0 collective-permute-done.16
  922.3 4.0 collective-permute-done.17
  927.1 4.1 collective-permute-start.19
  931.2 2.4 collective-permute-done.18
  934.2 2.0 multiply_reduce_fusion
  936.3 80.3 %psum.55 = f32[2,32]{1,0:T(2,128)S(1)} all-reduce(f32[2,32]{1,0:T(2,128)S(1)} %dynamic_update_slice.25), channel_id=1, replica_groups=mesh['blk'=32,'leaf'=4,'samp'=2] {'blk','leaf','samp'}, use_global_device_ids=true, to_apply=%region_18.23 | all-reduce | flops 64 | bytes 512 | tf_op jit(solution)/shard_map/psum | solution.py:84
  (168 shorter events, 60.4 us)
Async XLA Ops:
  7.2 393.1 %all-reduce.8.cloned.1.call-start = ((), (), s32[]{:S(2)}) async-start(), calls=%async_computation.1 | async-start | bytes 2359296 | tf_op jit(solution)/shard_map/psum | solution.py:95
  8.5 13.3 %collective-permute-start = (f32[512,256]{0,1:T(8,128)S(1)}, f32[512,256]{0,1:T(8,128)S(1)}, u32[]{:S(2)}, u32[]{:S(2)}) collective-permute-start(f32[512,256]{0,1:T(8,128)S(1)} %copy.10), channel_id=1, source_target_pairs={{0,2},{2,4},{4,6},{6,0},{1,3},{3,5},{5,7},{7,1},{8,10},{10,12},{12... | collective-permute-start | bytes 1572872 | tf_op jit(solution)/shard_map/ppermute | solution.py:41
  21.7 13.3 %collective-permute-start.1 = (f32[512,256]{0,1:T(8,128)S(1)}, f32[512,256]{0,1:T(8,128)S(1)}, u32[]{:S(2)}, u32[]{:S(2)}) collective-permute-start(f32[512,256]{0,1:T(8,128)S(1)} %collective-permute-done), channel_id=1, source_target_pairs={{0,2},{2,4},{4,6},{6,0},{1,3},{3,5},{5,7},{7,1},{8,10},{10,12},{12... | collective-permute-start | bytes 1572872 | tf_op jit(solution)/shard_map/ppermute | solution.py:41
  23.3 10.9 %collective-permute-start.5 = (f32[3,256]{1,0:T(4,128)}, f32[3,256]{1,0:T(4,128)S(1)}, u32[]{:S(2)}, u32[]{:S(2)}) collective-permute-start(f32[3,256]{1,0:T(4,128)} %param.13), channel_id=1, source_target_pairs={{0,2},{2,4},{4,6},{6,0},{1,3},{3,5},{5,7},{7,1},{8,10},{10,12},{12... | collective-permute-start | bytes 9224 | tf_op jit(solution)/shard_map/ppermute | solution.py:41
  34.2 3.7 collective-permute-start.6
  35.0 11.9 %collective-permute-start.2 = (f32[512,256]{0,1:T(8,128)S(1)}, f32[512,256]{0,1:T(8,128)S(1)}, u32[]{:S(2)}, u32[]{:S(2)}) collective-permute-start(f32[512,256]{0,1:T(8,128)S(1)} %collective-permute-done.1), channel_id=1, source_target_pairs={{0,2},{2,4},{4,6},{6,0},{1,3},{3,5},{5,7},{7,1},{8,10},{10,12},{12... | collective-permute-start | bytes 1572872 | tf_op jit(solution)/shard_map/ppermute | solution.py:41
  37.8 9.1 collective-permute-start.7
  47.3 11.5 %copy-start.10 = (f32[3,256]{1,0:T(4,128)S(1)}, f32[3,256]{1,0:T(4,128)}, u32[]{:S(2)}) copy-start(f32[3,256]{1,0:T(4,128)} %param.13) | copy-start | bytes 9220
  48.8 57.1 %collective-permute-start.3 = (f32[512,1024]{0,1:T(8,128)}, f32[512,1024]{0,1:T(8,128)}, u32[]{:S(2)}, u32[]{:S(2)}) collective-permute-start(f32[512,1024]{0,1:T(8,128)} %constant_dynamic-slice_fusion.6), channel_id=1, source_target_pairs={{248,0},{0,8},{8,16},{16,24},{24,32},{32,40},{40,48},{48,56},{56,6... | collective-permute-start | bytes 6291464 | tf_op jit(solution)/shard_map/ppermute | solution.py:17
  52.7 53.3 %collective-permute-start.4 = (f32[512,1024]{0,1:T(8,128)}, f32[512,1024]{0,1:T(8,128)}, u32[]{:S(2)}, u32[]{:S(2)}) collective-permute-start(f32[512,1024]{0,1:T(8,128)} %constant_dynamic-slice_fusion.6), channel_id=1, source_target_pairs={{8,0},{16,8},{24,16},{32,24},{40,32},{48,40},{56,48},{64,56},{72,6... | collective-permute-start | bytes 6291464 | tf_op jit(solution)/shard_map/ppermute | solution.py:17
  58.9 43.2 %collective-permute-start.8 = (f32[3,1024]{1,0:T(4,128)S(1)}, f32[3,1024]{1,0:T(4,128)S(1)}, u32[]{:S(2)}, u32[]{:S(2)}) collective-permute-start(f32[3,1024]{1,0:T(4,128)S(1)} %constant_dynamic-slice_fusion.5), channel_id=1, source_target_pairs={{248,0},{0,8},{8,16},{16,24},{24,32},{32,40},{40,48},{48,56},{56,6... | collective-permute-start | bytes 36872 | tf_op jit(solution)/shard_map/ppermute | solution.py:17
  59.0 43.1 %collective-permute-start.9 = (f32[3,1024]{1,0:T(4,128)S(1)}, f32[3,1024]{1,0:T(4,128)S(1)}, u32[]{:S(2)}, u32[]{:S(2)}) collective-permute-start(f32[3,1024]{1,0:T(4,128)S(1)} %constant_dynamic-slice_fusion.5), channel_id=1, source_target_pairs={{8,0},{16,8},{24,16},{32,24},{40,32},{48,40},{56,48},{64,56},{72,6... | collective-permute-start | bytes 36872 | tf_op jit(solution)/shard_map/ppermute | solution.py:17
  118.7 5.6 copy-start
  138.9 3.7 copy-start.4
  138.9 3.7 copy-start.11
  143.2 0.7 copy-start.6
  143.8 684.7 %all-reduce.6.cloned.1.call-start = ((), (), s32[]{:S(2)}) async-start(), calls=%async_computation | async-start | bytes 262144 | tf_op jit(solution)/shard_map/psum | solution.py:84
  404.6 1.0 copy-start.1
  456.2 94.5 %copy-start.8 = (f32[2,512,32]{1,2,0:T(8,128)S(1)}, f32[2,512,32]{1,2,0:T(8,128)}, u32[]{:S(2)}) copy-start(f32[2,512,32]{1,2,0:T(8,128)} %get-tuple-element.51) | copy-start | bytes 393220
  559.5 20.1 %copy-start.2 = (f32[32,256]{1,0:T(8,128)}, f32[32,256]{1,0:T(8,128)S(1)}, u32[]{:S(2)}) copy-start(f32[32,256]{1,0:T(8,128)S(1)} %convolution_subtract_fusion.4) | copy-start | bytes 98308
  559.5 4.2 collective-permute-start.10
  563.7 4.6 collective-permute-start.11
  568.3 4.0 collective-permute-start.12
  572.3 7.2 collective-permute-start.13
  572.4 7.1 collective-permute-start.14
  580.2 87.6 %copy-start.5 = (f32[32,256]{1,0:T(8,128)S(1)}, f32[32,256]{1,0:T(8,128)}, u32[]{:S(2)}) copy-start(f32[32,256]{1,0:T(8,128)} %param.17) | copy-start | bytes 98308
  580.2 248.3 %copy-start.9 = (f32[2,512,32]{1,2,0:T(8,128)S(1)}, f32[2,512,32]{1,2,0:T(8,128)}, u32[]{:S(2)}) copy-start(f32[2,512,32]{1,2,0:T(8,128)} %get-tuple-element.51) | copy-start | bytes 393220
  583.1 331.2 %copy-start.3 = (f32[32,256]{1,0:T(8,128)S(1)}, f32[32,256]{1,0:T(8,128)}, u32[]{:S(2)}) copy-start(f32[32,256]{1,0:T(8,128)} %copy-done.2) | copy-start | bytes 98308
  583.7 0.6 copy-start.7
  914.3 4.0 collective-permute-start.15
  918.3 4.0 collective-permute-start.16
  922.3 4.0 collective-permute-start.17
  926.4 7.2 collective-permute-start.18
  927.1 6.5 collective-permute-start.19
Sparse Core Ops, SparseCore 0:
  144.0 256.2 all-reduce.7
  584.5 244.0 all-reduce.5
